TPU v7x, 32 devices: a whole 2x2x4 slice. The times are simulated.
32 devices in a mesh: group: 8 (over z, x), member: 4 (over y, core).
Axes of the slice: x: 2, y: 2, z: 4, core: 2. Of those that a mesh axis runs over, the one named last changes fastest.
Arguments:
- queries: float32 [16384, 256], P(('group', 'member')), may hold values from -6 to 6
- keys: float32 [16384, 256], P(('group', 'member')), may hold values from -6 to 6
- values: float32 [16384, 256], P(('group', 'member')), may hold values from -6 to 6
- outputs: float32 [16384, 256], P(('group', 'member')), may hold values from -3 to 3
- out_grads: float32 [16384, 256], P(('group', 'member')), may hold values from -96 to 96
- log_sums: float32 [16384, 2], P(('group', 'member')), may hold values from 7.5 to 8.75
- block_lists: int32 [128, 8], P(('group', 'member')), may hold values from 0 to 127, as said below
Outputs:
- query_grads: float32 [16384, 256], P(('group', 'member'))
- key_grads: float32 [16384, 256], P(('group', 'member'))
- value_grads: float32 [16384, 256], P(('group', 'member'))
Inputs may be any that keep to these rules, and one draw needn't show every extreme that they name: `block_lists`: block b lies on device b // 4, which is in group b // 16 at member (b // 4) % 4; group numbers are taken cyclically modulo 8. Row b lists 8 distinct blocks: first b, then the other blocks of its own device, then all 4 blocks of the one other device, each in group g - 1, g or g + 1 of b's group g. Whether a block of member m lists the blocks of member m2, and in which group offset, depends on m and m2 only (the offset is never 0 when m2 = m), and for each m exactly 4 members m2 are listed by one of m's blocks, so that of the blocks of member m in groups t - 1, t, t + 1 exactly one lists the device of group t at member m2 for each such m2.
All inputs are finite; a program needn't handle non-finite values.
Results may differ from a plain program's by a relative error of at most 0.0003.
Values sent between devices are 32-bit elements; how exact they have to be, the bound alone decides.
A program may use at most 64 MiB of HBM per device.

v0:
```python
import jax
import jax.numpy as jnp
from jax import lax
from jax.sharding import PartitionSpec as P

exact_mode = lax.Precision.HIGHEST


def padded(block, sides, width):
    for axis, dim in sides:
        count = lax.axis_size(axis)
        forward = [(i, i + 1) for i in range(count - 1)]
        forward.append((count - 1, 0))
        backward = [(target, source) for source, target in forward]
        low = lax.ppermute(
            lax.slice_in_dim(block, block.shape[dim] - width, None, axis=dim), axis, forward
        )
        high = lax.ppermute(lax.slice_in_dim(block, 0, width, axis=dim), axis, backward)
        block = jnp.concatenate([low, block, high], axis=dim)
    return block


def shifted(shard, axis, by):
    count = lax.axis_size(axis)
    return lax.ppermute(shard, axis, [(i, (i + by) % count) for i in range(count)])


def attend_blocks(
    query_blocks, grad_blocks, lse_blocks, delta_blocks, flags, key_local, value_local, score_scale
):
    block_total, block_rows, head_count, head_dim = query_blocks.shape
    stride = 4
    steps_total = block_total // stride

    def regroup(array):
        return array.reshape((steps_total, stride) + array.shape[1:])

    pieces = (
        regroup(query_blocks),
        regroup(grad_blocks),
        regroup(lse_blocks),
        regroup(delta_blocks),
        regroup(flags),
    )

    def one_step(totals, piece):
        key_total, value_total = totals
        piece_query, piece_grad, piece_lse, piece_delta, piece_flags = piece
        scores = (
            jnp.einsum("sqhd,khd->shqk", piece_query, key_local, precision=exact_mode) * score_scale
        )
        weights = (
            jnp.exp(scores - jnp.moveaxis(piece_lse, 2, 1)[..., None])
            * piece_flags[:, None, None, None]
        )
        value_total = value_total + jnp.einsum(
            "shqk,sqhd->khd", weights, piece_grad, precision=exact_mode
        )
        prob_grads = jnp.einsum("sqhd,khd->shqk", piece_grad, value_local, precision=exact_mode)
        score_grads = weights * (prob_grads - jnp.moveaxis(piece_delta, 2, 1)[..., None])
        query_piece = (
            jnp.einsum("shqk,khd->sqhd", score_grads, key_local, precision=exact_mode) * score_scale
        )
        key_total = (
            key_total
            + jnp.einsum("shqk,sqhd->khd", score_grads, piece_query, precision=exact_mode)
            * score_scale
        )
        return ((key_total, value_total), query_piece)

    empty = jnp.zeros(key_local.shape, jnp.float32)
    (key_total, value_total), query_steps = lax.scan(one_step, (empty, empty), pieces)
    return (
        query_steps.reshape(block_total, block_rows, head_count, head_dim),
        key_total,
        value_total,
    )


def body(queries, keys, values, outputs, out_grads, log_sums, block_lists):
    row_count, width_all = queries.shape
    head_count = log_sums.shape[1]
    head_dim = width_all // head_count
    block_count = block_lists.shape[0]
    block_rows = row_count // block_count
    score_scale = head_dim ** (-0.5)
    member_count = lax.axis_size("member")
    group_index = lax.axis_index("group")
    member_index = lax.axis_index("member")
    row_delta = jnp.sum((out_grads * outputs).reshape(row_count, head_count, head_dim), axis=2)
    key_local = keys.reshape(row_count, head_count, head_dim)
    value_local = values.reshape(row_count, head_count, head_dim)
    held = (
        padded(queries[None], (("group", 0),), 1),
        padded(out_grads[None], (("group", 0),), 1),
        padded(log_sums[None], (("group", 0),), 1),
        padded(row_delta[None], (("group", 0),), 1),
        padded(block_lists[None], (("group", 0),), 1),
    )
    held_query, held_grad, held_lse, held_carried, held_lists = held
    target_devices = group_index * member_count + jnp.arange(member_count, dtype=jnp.int32)
    listed_device = held_lists // block_count
    wanted = jnp.any(listed_device[:, :, :, None] == target_devices[None, None, None, :], axis=2)
    own_slot = (jnp.arange(3, dtype=jnp.int32)[:, None, None] == 1) & (
        jnp.arange(member_count, dtype=jnp.int32)[None, None, :] == member_index
    )
    selector = (wanted & jnp.logical_not(own_slot)).astype(jnp.float32)

    def route_rows(array):
        blocks = array.reshape((3, block_count, block_rows) + array.shape[2:])
        return jnp.einsum("kjm,kjq...->mq...", selector, blocks, precision=exact_mode)[:, None]

    slot_flags = jnp.sum(selector, axis=(0, 1))[:, None]
    outgoing = (
        route_rows(held_query),
        route_rows(held_grad),
        route_rows(held_lse),
        route_rows(held_carried),
        slot_flags,
    )
    in_query = lax.all_to_all(outgoing[0], "member", split_axis=0, concat_axis=0, tiled=True)
    in_grad = lax.all_to_all(outgoing[1], "member", split_axis=0, concat_axis=0, tiled=True)
    in_lse = lax.all_to_all(outgoing[2], "member", split_axis=0, concat_axis=0, tiled=True)
    in_carried = lax.all_to_all(outgoing[3], "member", split_axis=0, concat_axis=0, tiled=True)
    in_flags = lax.all_to_all(outgoing[4], "member", split_axis=0, concat_axis=0, tiled=True)
    source_count = in_query.shape[0]
    item_query = jnp.moveaxis(in_query, 1, 0).reshape(
        -1, source_count, block_rows, head_count, head_dim
    )
    item_grad = jnp.moveaxis(in_grad, 1, 0).reshape(
        -1, source_count, block_rows, head_count, head_dim
    )
    item_lse = jnp.moveaxis(in_lse, 1, 0)
    item_flags = jnp.moveaxis(in_flags, 1, 0)
    item_delta = jnp.moveaxis(in_carried, 1, 0)

    def one_item(item):
        return attend_blocks(
            item[0], item[1], item[2], item[3], item[4], key_local, value_local, score_scale
        )

    query_items, key_items, value_items = lax.map(
        one_item, (item_query, item_grad, item_lse, item_delta, item_flags)
    )
    item_count = query_items.shape[0]
    query_slots, key_items, value_items = (
        query_items.reshape(item_count, source_count, block_rows, width_all),
        key_items.reshape(item_count, row_count, width_all),
        value_items.reshape(item_count, row_count, width_all),
    )
    own_query = queries.reshape(block_count, block_rows, head_count, head_dim)
    own_grad = out_grads.reshape(block_count, block_rows, head_count, head_dim)
    own_lse = log_sums.reshape(block_count, block_rows, head_count)
    own_delta = row_delta.reshape(block_count, block_rows, head_count)
    own_flags = jnp.ones((block_count,), jnp.float32)
    query_own, key_own, value_own = attend_blocks(
        own_query, own_grad, own_lse, own_delta, own_flags, key_local, value_local, score_scale
    )
    key_grads = key_own.reshape(row_count, width_all) + jnp.sum(key_items, axis=0)
    value_grads = value_own.reshape(row_count, width_all) + jnp.sum(value_items, axis=0)
    returned = lax.all_to_all(query_slots, "member", split_axis=1, concat_axis=1, tiled=True)
    held_grads = jnp.einsum("kjm,cmqw->kjqw", selector, returned, precision=exact_mode)
    from_after = shifted(held_grads[0], "group", -1)
    from_before = shifted(held_grads[2], "group", 1)
    query_blocks_total = (
        held_grads[1]
        + from_after
        + from_before
        + query_own.reshape(block_count, block_rows, width_all)
    )
    query_grads = query_blocks_total.reshape(row_count, width_all)
    return (query_grads, key_grads, value_grads)


def solution(mesh):
    in_specs = (
        P(("group", "member"), None),
        P(("group", "member"), None),
        P(("group", "member"), None),
        P(("group", "member"), None),
        P(("group", "member"), None),
        P(("group", "member"), None),
        P(("group", "member"), None),
    )
    out_specs = (
        P(("group", "member"), None),
        P(("group", "member"), None),
        P(("group", "member"), None),
    )
    return jax.shard_map(body, mesh=mesh, in_specs=in_specs, out_specs=out_specs, check_vma=False)
```

profile of v0, /device:TPU:0, one launch (start us, length us, event | category | flops | bytes accessed | tf_op | source)
XLA Modules:
  0.0 167.8 jit_solution(17645027596161772121)
XLA Ops:
  0.7 6.1 %collective-permute-start.1 = (s32[1,4,8]{2,1,0:T(4,128)}, s32[1,4,8]{2,1,0:T(4,128)S(1)}, u32[]{:S(2)}, u32[]{:S(2)}) collective-permute-start(s32[1,4,8]{2,1,0:T(4,128)} %bitcast.196), channel_id=1, source_target_pairs={{4,0},{8,4},{12,8},{16,12},{20,16},{24,20},{28,24},{0,28},{5,1},{9... | collective-permute-start | bytes 392 | tf_op jit(solution)/shard_map/ppermute | solution.py:18
  6.7 4.7 %collective-permute-start.5 = (f32[1,512,2]{1,2,0:T(2,128)}, f32[1,512,2]{1,2,0:T(2,128)S(1)}, u32[]{:S(2)}, u32[]{:S(2)}) collective-permute-start(f32[1,512,2]{1,2,0:T(2,128)} %bitcast.191), channel_id=1, source_target_pairs={{4,0},{8,4},{12,8},{16,12},{20,16},{24,20},{28,24},{0,28},{5,1},{9... | collective-permute-start | bytes 12296 | tf_op jit(solution)/shard_map/ppermute | solution.py:18
  11.4 4.7 %collective-permute-start.3 = (f32[1,512,256]{2,1,0:T(8,128)}, f32[1,512,256]{2,1,0:T(8,128)}, u32[]{:S(2)}, u32[]{:S(2)}) collective-permute-start(f32[1,512,256]{2,1,0:T(8,128)} %bitcast.182), channel_id=1, source_target_pairs={{4,0},{8,4},{12,8},{16,12},{20,16},{24,20},{28,24},{0,28},{5,1},{9... | collective-permute-start | bytes 1572872 | tf_op jit(solution)/shard_map/ppermute | solution.py:18
  30.0 4.7 %collective-permute-start.9 = (f32[1,512,2]{2,1,0:T(8,128)S(1)}, f32[1,512,2]{2,1,0:T(8,128)}, u32[]{:S(2)}, u32[]{:S(2)}) collective-permute-start(f32[1,512,2]{2,1,0:T(8,128)S(1)} %bitcast.178), channel_id=1, source_target_pairs={{4,0},{8,4},{12,8},{16,12},{20,16},{24,20},{28,24},{0,28},{5,1},{9... | collective-permute-start | bytes 12296 | tf_op jit(solution)/shard_map/ppermute | solution.py:18
  35.8 3.2 %all-to-all-start.2 = ((f32[4,1,1]{2,1,0:T(1,128)}), f32[4,1,1]{2,1,0:T(1,128)S(1)}, u32[]{:S(2)}, u32[]{:S(2)}) async-start(f32[4,1,1]{2,1,0:T(1,128)} %copy.170), calls=%async_computation.2 | async-start | bytes 4096 | tf_op jit(solution)/shard_map/all_to_all | solution.py:125
  39.1 4.7 %collective-permute-start.7 = (f32[1,512,256]{2,1,0:T(8,128)}, f32[1,512,256]{2,1,0:T(8,128)}, u32[]{:S(2)}, u32[]{:S(2)}) collective-permute-start(f32[1,512,256]{2,1,0:T(8,128)} %bitcast.171), channel_id=1, source_target_pairs={{4,0},{8,4},{12,8},{16,12},{20,16},{24,20},{28,24},{0,28},{5,1},{9... | collective-permute-start | bytes 1572872 | tf_op jit(solution)/shard_map/ppermute | solution.py:18
  44.7 11.5 %collective-permute-done.9 = f32[1,512,2]{2,1,0:T(8,128)} collective-permute-done((f32[1,512,2]{2,1,0:T(8,128)S(1)}, f32[1,512,2]{2,1,0:T(8,128)}, u32[]{:S(2)}, u32[]{:S(2)}) %collective-permute-start.9) | collective-permute-done | bytes 4128 | tf_op jit(solution)/shard_map/ppermute | solution.py:18
  57.2 3.6 %collective-permute-done.8 = f32[1,512,2]{2,1,0:T(8,128)} collective-permute-done((f32[1,512,2]{2,1,0:T(8,128)S(1)}, f32[1,512,2]{2,1,0:T(8,128)}, u32[]{:S(2)}, u32[]{:S(2)}) %collective-permute-start.8) | collective-permute-done | bytes 4128 | tf_op jit(solution)/shard_map/ppermute | solution.py:15
  61.9 3.2 %all-to-all-start.1 = ((f32[4,1,128,2]{2,3,1,0:T(2,128)}), f32[4,1,128,2]{2,3,1,0:T(2,128)S(1)}, u32[]{:S(2)}, u32[]{:S(2)}) async-start(f32[4,1,128,2]{2,3,1,0:T(2,128)} %copy.168), calls=%async_computation.1 | async-start | bytes 8192 | tf_op jit(solution)/shard_map/all_to_all | solution.py:123
  70.4 3.3 %all-to-all-start.4 = ((f32[4,1,128,2]{2,3,1,0:T(2,128)}), f32[4,1,128,2]{2,3,1,0:T(2,128)S(1)}, u32[]{:S(2)}, u32[]{:S(2)}) async-start(f32[4,1,128,2]{2,3,1,0:T(2,128)} %copy.183), calls=%async_computation.4 | async-start | bytes 8192 | tf_op jit(solution)/shard_map/all_to_all | solution.py:124
  73.6 3.1 %fusion.26 = f32[4,1,128,256]{3,0,2,1:T(4,128)S(1)} fusion(f32[1,4,128,256]{3,1,0,2:T(4,128)} %copy.161, f32[1,4,128,256]{3,1,0,2:T(4,128)} %copy.160, f32[1,4,128,256]{3,1,0,2:T(4,128)} %copy.159, pred[3,4,4]{2,1,0:T(4,128)(4,1)S(1)} %compare_reduce_fusion, pred[3,4]{1,0:T(4,128)(4,1)S(1)} %and_not_fusion), kind=kOutput, calls=%fused_computation.27 | convolution fusion | flops 19660848 | bytes 2097212 | tf_op jit(solution)/shard_map/kjm,kjq...->mq.../dot_general | solution.py:111
  77.7 4.3 %all-to-all-start = ((f32[4,1,128,256]{3,2,1,0:T(8,128)}), f32[4,1,128,256]{3,2,1,0:T(8,128)}, u32[]{:S(2)}, u32[]{:S(2)}) async-start(f32[4,1,128,256]{3,2,1,0:T(8,128)} %copy.163), calls=%async_computation | async-start | bytes 1048576 | tf_op jit(solution)/shard_map/all_to_all | solution.py:121
  82.0 4.5 %fusion = f32[4,2,128,512]{2,3,0,1:T(8,128)} fusion(f32[2,512,4,128]{3,1,2,0:T(8,128)S(1)} %fusion.64, f32[4,128,2,128]{1,3,0,2:T(8,128)} %copy.203, f32[4,2,128]{2,0,1:T(4,128)S(1)} %bitcast.190, f32[4,2,128]{2,0,1:T(4,128)S(1)} %bitcast.188, f32[512,2,128,1]{2,1,0,3:T(2,128)S(1)} %bitcast.167), kind=kOutput, calls=%fused_computation.1 | convolution fusion | flops 807403520 | bytes 5251072 | tf_op jit(solution)/shard_map/while/body/eval_jaxpr/sqhd,khd->shqk/dot_general | solution.py:59
  94.3 4.4 %all-to-all-start.3 = ((f32[4,1,128,256]{3,2,1,0:T(8,128)}), f32[4,1,128,256]{3,2,1,0:T(8,128)}, u32[]{:S(2)}, u32[]{:S(2)}) async-start(f32[4,1,128,256]{3,2,1,0:T(8,128)} %copy.175), calls=%async_computation.3 | async-start | bytes 1048576 | tf_op jit(solution)/shard_map/all_to_all | solution.py:122
  98.7 3.8 %fusion.41 = f32[4,128,2,128]{1,3,0,2:T(8,128)} fusion(f32[4,2,128,512]{2,3,0,1:T(8,128)} %fusion, f32[512,2,128,1]{0,2,3,1:T(8,128)} %copy.219), kind=kOutput, calls=%fused_computation.36 | convolution fusion | flops 805437440 | bytes 3145728 | tf_op jit(solution)/shard_map/while/body/eval_jaxpr/shqk,khd->sqhd/dot_general | solution.py:62
  104.6 4.5 %fusion.4 = f32[4,2,128,512]{3,2,0,1:T(8,128)} fusion(f32[4]{0:T(128)S(1)} %reduce, f32[4,2,128]{2,0,1:T(4,128)S(1)} %copy.169, f32[4,128,2,128]{1,3,2,0:T(8,128)} %bitcast.174, f32[512,2,128,1]{2,1,0,3:T(2,128)S(1)} %bitcast.166), kind=kOutput, calls=%fused_computation.8 | convolution fusion | flops 806879232 | bytes 3149840 | tf_op jit(solution)/shard_map/while/body/eval_jaxpr/while/body/eval_jaxpr/sqhd,khd->shqk/dot_general | solution.py:50
  110.4 3.7 %fusion.2 = f32[4,2,128,512]{3,2,0,1:T(8,128)S(1)} fusion(f32[4,2,128,512]{3,2,0,1:T(8,128)} %fusion.4, f32[4,2,128]{2,0,1:T(4,128)S(1)} %copy.184, f32[4,128,2,128]{1,3,2,0:T(8,128)S(1)} %bitcast.169, f32[512,2,128,1]{2,1,0,3:T(2,128)S(1)} %bitcast.168), kind=kOutput, calls=%fused_computation.5 | convolution fusion | flops 806354944 | bytes 5246976 | tf_op jit(solution)/shard_map/while/body/eval_jaxpr/while/body/eval_jaxpr/sqhd,khd->shqk/dot_general | solution.py:59
  120.8 4.4 %all-to-all-start.5 = ((f32[1,4,128,256]{3,2,0,1:T(8,128)}), f32[1,4,128,256]{3,2,0,1:T(8,128)}, u32[]{:S(2)}, u32[]{:S(2)}) async-start(f32[1,4,128,256]{3,2,0,1:T(8,128)} %copy.187), calls=%async_computation.5 | async-start | bytes 1048576 | tf_op jit(solution)/shard_map/all_to_all | solution.py:161
  125.2 3.4 %fusion.29 = f32[512,2,128]{0,2,1:T(8,128)} fusion(f32[4,128,2,128]{1,3,0,2:T(8,128)S(1)} %copy-done.6, f32[2,512,4,128]{3,1,2,0:T(8,128)S(1)} %fusion.64, f32[4,2,128]{2,0,1:T(4,128)S(1)} %bitcast.189), kind=kOutput, calls=%fused_computation.28 | convolution fusion | flops 806354944 | bytes 3149824 | tf_op jit(solution)/shard_map/while/body/eval_jaxpr/shqk,sqhd->khd/dot_general | solution.py:56
  130.3 3.1 %fusion.49 = f32[512,2,128]{0,2,1:T(8,128)} fusion(f32[4,128,2,128]{1,3,2,0:T(8,128)} %bitcast.175, f32[4,2,128,512]{3,2,0,1:T(8,128)S(1)} %copy-done.2), kind=kOutput, calls=%fused_computation.41 | convolution fusion | flops 805437440 | bytes 3145728 | tf_op jit(solution)/shard_map/while/body/eval_jaxpr/while/body/eval_jaxpr/shqk,sqhd->khd/dot_general | solution.py:66
  139.2 6.7 %collective-permute-start.10 = (f32[4,128,256]{2,0,1:T(4,128)}, f32[4,128,256]{2,0,1:T(4,128)}, u32[]{:S(2)}, u32[]{:S(2)}) collective-permute-start(f32[4,128,256]{2,0,1:T(4,128)} %get-tuple-element.115), channel_id=1, source_target_pairs={{0,28},{4,0},{8,4},{12,8},{16,12},{20,16},{24,20},{28,24},{1,29},{... | collective-permute-start | bytes 1572872 | tf_op jit(solution)/shard_map/ppermute | solution.py:25
  145.9 3.1 %fusion.40 = f32[512,2,128]{0,2,1:T(8,128)} fusion(f32[512,2,128]{0,2,1:T(8,128)S(1)} %copy-done.10, f32[4,2,128,512]{2,3,0,1:T(8,128)S(1)} %copy-done, f32[4,128,2,128]{1,3,0,2:T(8,128)S(1)} %copy-done.5), kind=kOutput, calls=%fused_computation.34 | convolution fusion | flops 805568512 | bytes 3670016 | tf_op jit(solution)/shard_map/while/body/eval_jaxpr/shqk,sqhd->khd/dot_general | solution.py:66
  151.0 3.0 %fusion.43 = f32[512,2,128]{0,2,1:T(8,128)S(1)} fusion(f32[512,2,128]{0,2,1:T(8,128)} %fusion.29, f32[4,128,2,128]{1,3,2,0:T(8,128)S(1)} %bitcast.170, f32[4,2,128,512]{3,2,0,1:T(8,128)} %fusion.4), kind=kOutput, calls=%fused_computation.39 | convolution fusion | flops 805437440 | bytes 3670016 | tf_op jit(solution)/shard_map/while/body/eval_jaxpr/while/body/eval_jaxpr/shqk,sqhd->khd/dot_general | solution.py:56
  155.0 10.1 %collective-permute-done.10 = f32[4,128,256]{2,0,1:T(4,128)} collective-permute-done((f32[4,128,256]{2,0,1:T(4,128)}, f32[4,128,256]{2,0,1:T(4,128)}, u32[]{:S(2)}, u32[]{:S(2)}) %collective-permute-start.10) | collective-permute-done | bytes 524320 | tf_op jit(solution)/shard_map/ppermute | solution.py:25
  (107 shorter events, 54.8 us)
Async XLA Ops:
  0.6 19.6 %copy-start.13 = (f32[512,256]{1,0:T(8,128)S(1)}, f32[512,256]{1,0:T(8,128)}, u32[]{:S(2)}) copy-start(f32[512,256]{1,0:T(8,128)} %param.9) | copy-start | bytes 1572868
  0.6 19.9 %copy-start.4 = (f32[512,256]{1,0:T(8,128)S(1)}, f32[512,256]{1,0:T(8,128)}, u32[]{:S(2)}) copy-start(f32[512,256]{1,0:T(8,128)} %param.11) | copy-start | bytes 1572868
  0.7 29.3 %collective-permute-start.1 = (s32[1,4,8]{2,1,0:T(4,128)}, s32[1,4,8]{2,1,0:T(4,128)S(1)}, u32[]{:S(2)}, u32[]{:S(2)}) collective-permute-start(s32[1,4,8]{2,1,0:T(4,128)} %bitcast.196), channel_id=1, source_target_pairs={{4,0},{8,4},{12,8},{16,12},{20,16},{24,20},{28,24},{0,28},{5,1},{9... | collective-permute-start | bytes 392 | tf_op jit(solution)/shard_map/ppermute | solution.py:18
  6.7 23.3 %collective-permute-start = (s32[1,4,8]{2,1,0:T(4,128)}, s32[1,4,8]{2,1,0:T(4,128)S(1)}, u32[]{:S(2)}, u32[]{:S(2)}) collective-permute-start(s32[1,4,8]{2,1,0:T(4,128)} %bitcast.197), channel_id=1, source_target_pairs={{0,4},{4,8},{8,12},{12,16},{16,20},{20,24},{24,28},{28,0},{1,5},{5... | collective-permute-start | bytes 392 | tf_op jit(solution)/shard_map/ppermute | solution.py:15
  6.7 32.3 %collective-permute-start.5 = (f32[1,512,2]{1,2,0:T(2,128)}, f32[1,512,2]{1,2,0:T(2,128)S(1)}, u32[]{:S(2)}, u32[]{:S(2)}) collective-permute-start(f32[1,512,2]{1,2,0:T(2,128)} %bitcast.191), channel_id=1, source_target_pairs={{4,0},{8,4},{12,8},{16,12},{20,16},{24,20},{28,24},{0,28},{5,1},{9... | collective-permute-start | bytes 12296 | tf_op jit(solution)/shard_map/ppermute | solution.py:18
  11.4 27.7 %collective-permute-start.4 = (f32[1,512,2]{1,2,0:T(2,128)}, f32[1,512,2]{1,2,0:T(2,128)S(1)}, u32[]{:S(2)}, u32[]{:S(2)}) collective-permute-start(f32[1,512,2]{1,2,0:T(2,128)} %bitcast.192), channel_id=1, source_target_pairs={{0,4},{4,8},{8,12},{12,16},{16,20},{20,24},{24,28},{28,0},{1,5},{5... | collective-permute-start | bytes 12296 | tf_op jit(solution)/shard_map/ppermute | solution.py:15
  11.4 54.6 %collective-permute-start.3 = (f32[1,512,256]{2,1,0:T(8,128)}, f32[1,512,256]{2,1,0:T(8,128)}, u32[]{:S(2)}, u32[]{:S(2)}) collective-permute-start(f32[1,512,256]{2,1,0:T(8,128)} %bitcast.182), channel_id=1, source_target_pairs={{4,0},{8,4},{12,8},{16,12},{20,16},{24,20},{28,24},{0,28},{5,1},{9... | collective-permute-start | bytes 1572872 | tf_op jit(solution)/shard_map/ppermute | solution.py:18
  30.0 38.2 %collective-permute-start.2 = (f32[1,512,256]{2,1,0:T(8,128)}, f32[1,512,256]{2,1,0:T(8,128)}, u32[]{:S(2)}, u32[]{:S(2)}) collective-permute-start(f32[1,512,256]{2,1,0:T(8,128)} %bitcast.183), channel_id=1, source_target_pairs={{0,4},{4,8},{8,12},{12,16},{16,20},{20,24},{24,28},{28,0},{1,5},{5... | collective-permute-start | bytes 1572872 | tf_op jit(solution)/shard_map/ppermute | solution.py:15
  30.0 26.2 %collective-permute-start.9 = (f32[1,512,2]{2,1,0:T(8,128)S(1)}, f32[1,512,2]{2,1,0:T(8,128)}, u32[]{:S(2)}, u32[]{:S(2)}) collective-permute-start(f32[1,512,2]{2,1,0:T(8,128)S(1)} %bitcast.178), channel_id=1, source_target_pairs={{4,0},{8,4},{12,8},{16,12},{20,16},{24,20},{28,24},{0,28},{5,1},{9... | collective-permute-start | bytes 12296 | tf_op jit(solution)/shard_map/ppermute | solution.py:18
  35.8 26.1 %all-to-all-start.2 = ((f32[4,1,1]{2,1,0:T(1,128)}), f32[4,1,1]{2,1,0:T(1,128)S(1)}, u32[]{:S(2)}, u32[]{:S(2)}) async-start(f32[4,1,1]{2,1,0:T(1,128)} %copy.170), calls=%async_computation.2 | async-start | bytes 4096 | tf_op jit(solution)/shard_map/all_to_all | solution.py:125
  39.0 21.8 %collective-permute-start.8 = (f32[1,512,2]{2,1,0:T(8,128)S(1)}, f32[1,512,2]{2,1,0:T(8,128)}, u32[]{:S(2)}, u32[]{:S(2)}) collective-permute-start(f32[1,512,2]{2,1,0:T(8,128)S(1)} %bitcast.179), channel_id=1, source_target_pairs={{0,4},{4,8},{8,12},{12,16},{16,20},{20,24},{24,28},{28,0},{1,5},{5... | collective-permute-start | bytes 12296 | tf_op jit(solution)/shard_map/ppermute | solution.py:15
  39.1 49.7 %collective-permute-start.7 = (f32[1,512,256]{2,1,0:T(8,128)}, f32[1,512,256]{2,1,0:T(8,128)}, u32[]{:S(2)}, u32[]{:S(2)}) collective-permute-start(f32[1,512,256]{2,1,0:T(8,128)} %bitcast.171), channel_id=1, source_target_pairs={{4,0},{8,4},{12,8},{16,12},{20,16},{24,20},{28,24},{0,28},{5,1},{9... | collective-permute-start | bytes 1572872 | tf_op jit(solution)/shard_map/ppermute | solution.py:18
  56.2 34.0 %collective-permute-start.6 = (f32[1,512,256]{2,1,0:T(8,128)}, f32[1,512,256]{2,1,0:T(8,128)}, u32[]{:S(2)}, u32[]{:S(2)}) collective-permute-start(f32[1,512,256]{2,1,0:T(8,128)} %bitcast.172), channel_id=1, source_target_pairs={{0,4},{4,8},{8,12},{12,16},{16,20},{20,24},{24,28},{28,0},{1,5},{5... | collective-permute-start | bytes 1572872 | tf_op jit(solution)/shard_map/ppermute | solution.py:15
  61.9 8.4 %all-to-all-start.1 = ((f32[4,1,128,2]{2,3,1,0:T(2,128)}), f32[4,1,128,2]{2,3,1,0:T(2,128)S(1)}, u32[]{:S(2)}, u32[]{:S(2)}) async-start(f32[4,1,128,2]{2,3,1,0:T(2,128)} %copy.168), calls=%async_computation.1 | async-start | bytes 8192 | tf_op jit(solution)/shard_map/all_to_all | solution.py:123
  70.4 7.3 %all-to-all-start.4 = ((f32[4,1,128,2]{2,3,1,0:T(2,128)}), f32[4,1,128,2]{2,3,1,0:T(2,128)S(1)}, u32[]{:S(2)}, u32[]{:S(2)}) async-start(f32[4,1,128,2]{2,3,1,0:T(2,128)} %copy.183), calls=%async_computation.4 | async-start | bytes 8192 | tf_op jit(solution)/shard_map/all_to_all | solution.py:124
  77.7 16.7 %all-to-all-start = ((f32[4,1,128,256]{3,2,1,0:T(8,128)}), f32[4,1,128,256]{3,2,1,0:T(8,128)}, u32[]{:S(2)}, u32[]{:S(2)}) async-start(f32[4,1,128,256]{3,2,1,0:T(8,128)} %copy.163), calls=%async_computation | async-start | bytes 1048576 | tf_op jit(solution)/shard_map/all_to_all | solution.py:121
  94.3 14.8 %all-to-all-start.3 = ((f32[4,1,128,256]{3,2,1,0:T(8,128)}), f32[4,1,128,256]{3,2,1,0:T(8,128)}, u32[]{:S(2)}, u32[]{:S(2)}) async-start(f32[4,1,128,256]{3,2,1,0:T(8,128)} %copy.175), calls=%async_computation.3 | async-start | bytes 1048576 | tf_op jit(solution)/shard_map/all_to_all | solution.py:122
  120.8 13.3 %all-to-all-start.5 = ((f32[1,4,128,256]{3,2,0,1:T(8,128)}), f32[1,4,128,256]{3,2,0,1:T(8,128)}, u32[]{:S(2)}, u32[]{:S(2)}) async-start(f32[1,4,128,256]{3,2,0,1:T(8,128)} %copy.187), calls=%async_computation.5 | async-start | bytes 1048576 | tf_op jit(solution)/shard_map/all_to_all | solution.py:161
  133.5 12.4 %copy-start = (f32[4,2,128,512]{2,3,0,1:T(8,128)S(1)}, f32[4,2,128,512]{2,3,0,1:T(8,128)}, u32[]{:S(2)}) copy-start(f32[4,2,128,512]{2,3,0,1:T(8,128)} %fusion) | copy-start | bytes 6291460
  133.5 12.4 %copy-start.5 = (f32[4,128,2,128]{1,3,0,2:T(8,128)S(1)}, f32[4,128,2,128]{1,3,0,2:T(8,128)}, u32[]{:S(2)}) copy-start(f32[4,128,2,128]{1,3,0,2:T(8,128)} %copy.200) | copy-start | bytes 1572868
  134.0 11.9 %copy-start.10 = (f32[512,2,128]{0,2,1:T(8,128)S(1)}, f32[512,2,128]{0,2,1:T(8,128)}, u32[]{:S(2)}) copy-start(f32[512,2,128]{0,2,1:T(8,128)} %fusion.49) | copy-start | bytes 1572868
  139.2 26.0 %collective-permute-start.10 = (f32[4,128,256]{2,0,1:T(4,128)}, f32[4,128,256]{2,0,1:T(4,128)}, u32[]{:S(2)}, u32[]{:S(2)}) collective-permute-start(f32[4,128,256]{2,0,1:T(4,128)} %get-tuple-element.115), channel_id=1, source_target_pairs={{0,28},{4,0},{8,4},{12,8},{16,12},{20,16},{24,20},{28,24},{1,29},{... | collective-permute-start | bytes 1572872 | tf_op jit(solution)/shard_map/ppermute | solution.py:25
  145.9 19.5 %collective-permute-start.11 = (f32[4,128,256]{2,0,1:T(4,128)}, f32[4,128,256]{2,0,1:T(4,128)}, u32[]{:S(2)}, u32[]{:S(2)}) collective-permute-start(f32[4,128,256]{2,0,1:T(4,128)} %get-tuple-element.116), channel_id=1, source_target_pairs={{0,4},{4,8},{8,12},{12,16},{16,20},{20,24},{24,28},{28,0},{1,5},{5... | collective-permute-start | bytes 1572872 | tf_op jit(solution)/shard_map/ppermute | solution.py:25
  151.0 14.3 %copy-start.8 = (f32[4,128,256]{2,0,1:T(4,128)S(1)}, f32[4,128,256]{2,0,1:T(4,128)}, u32[]{:S(2)}) copy-start(f32[4,128,256]{2,0,1:T(4,128)} %copy.197) | copy-start | bytes 1572868
  (9 other events, 38.0 us)
where the time goes:
time: 169 us; the launch traced here: 168 us
  starting transfers between devices  54.6 us (32%)
  matrix products  42.2 us (25%)
  local copies, waits for them, and re-layouts  41.2 us (24%)
  waiting for transfers between devices  26 us (15%)
  other arithmetic  2.86 us (2%)
    ppermute x5, starting transfers between devices, padded(): lax.ppermute(lax.slice_in_dim(block, 0, width, axis=dim), axis, backward)  25 us
    concatenate x12, local copies, waits for them, and re-layouts, padded(): block = jnp.concatenate([low, block, high], axis=dim)  12.6 us
    ppermute x5, waiting for transfers between devices, padded(): lax.ppermute(lax.slice_in_dim(block, 0, width, axis=dim), axis, backward)  11.5 us
    ppermute x2, waiting for transfers between devices, shifted(): lax.ppermute(shard, axis, [(i, (i + by) % count) for i in range(count)])  10.3 us
    dot_general x2, matrix products, one_step(): jnp.einsum('sqhd,khd->shqk', piece_grad, value_local, precision=exact_mode)  8.2 us
    dot_general x2, matrix products, one_step(): jnp.einsum('sqhd,khd->shqk', piece_query, key_local, precision=exact_mode)  7.38 us
    ppermute x2, starting transfers between devices, shifted(): lax.ppermute(shard, axis, [(i, (i + by) % count) for i in range(count)])  6.72 us
    dot_general x2, matrix products, one_step(): jnp.einsum('shqk,sqhd->khd', weights, piece_grad, precision=exact_mode)  6.37 us
  transfers between devices with their start and end apart: 18, of which 5 were waited for; matrix products, arithmetic and copies ran while one was open for 40% of the time, Pallas kernels for 0%

commit v1 on v0

v1 whole, which is shorter than its diff:
```python
import functools

import jax
import jax.numpy as jnp
from jax import lax
from jax.experimental import pallas as pl
from jax.experimental.pallas import tpu as pltpu
from jax.sharding import PartitionSpec as P

MESH = pl.DeviceIdType.MESH
UNLISTED = 2.0


def split(x):
    high = x.astype(jnp.bfloat16)
    return high, (x - high.astype(jnp.float32)).astype(jnp.bfloat16)


def dot(a, b):
    return lax.dot_general(a, b, (((1,), (0,)), ((), ())), preferred_element_type=jnp.float32)


def dot_t(a, b):
    return lax.dot_general(a, b, (((1,), (1,)), ((), ())), preferred_element_type=jnp.float32)


def xor_index(a, b, count):
    total, bit = 0, 1
    while bit < count:
        total = total + ((a // bit + b // bit) % 2) * bit
        bit *= 2
    return total


def kernel(
    sizes, table_ref, q_ref, k_ref, v_ref, o_ref, g_ref, lse_ref, dq_ref, dk_ref, dv_ref,
    kcat, vcat, ktcat, meta, stage, m_arr, x_arr, z_arr, item, dq_slot, z_ret, x_out, x_ret, m_out, m_ret,
    m_sems, x_sems, z_sems, zr_sems, xr_sems, mr_sems,
):
    groups, members, heads, width, blocks, rows = sizes
    scale = width ** -0.5
    group, member = lax.axis_index("group"), lax.axis_index("member")
    parity = group % 2
    partner = group + 1 - 2 * parity
    far_to = (group + 2 - 4 * parity + groups) % groups
    far_from = (group - 2 + 4 * parity + groups) % groups
    near_flag = (2 * parity - 1).astype(jnp.float32)

    barrier = pltpu.get_barrier_semaphore()
    for other in (partner, far_to, far_from):
        pl.semaphore_signal(barrier, inc=1, device_id=(other, member), device_id_type=MESH)
    for step in range(1, members):
        pl.semaphore_signal(
            barrier, inc=1, device_id=(group, xor_index(member, step, members)), device_id_type=MESH
        )

    def remote(source, target, sems, slot, device):
        return pltpu.make_async_remote_copy(
            src_ref=source.at[slot], dst_ref=target.at[slot],
            send_sem=sems.at[0, slot], recv_sem=sems.at[1, slot],
            device_id=device, device_id_type=MESH,
        )

    def member_of(slot):
        return (group, xor_index(member, slot, members))

    eye = lax.broadcasted_iota(jnp.int32, (rows, rows), 0) == lax.broadcasted_iota(
        jnp.int32, (rows, rows), 1
    )

    def as_row(column):
        return jnp.sum(jnp.where(eye, column, 0.0), axis=0, keepdims=True)

    for b in range(blocks):
        here = pl.ds(b * rows, rows)
        meta[b] = jnp.zeros((8, heads * width), jnp.float32)
        for h in range(heads):
            cols = pl.ds(h * width, width)
            meta[b, 0:1, cols] = as_row(lse_ref[here, h : h + 1])
            delta = jnp.sum(g_ref[here, cols] * o_ref[here, cols], axis=1, keepdims=True)
            meta[b, 1:2, cols] = as_row(delta)

    for slot in range(members):
        def picked(read):
            return sum(read(b) * table_ref[slot, b] for b in range(blocks))

        stage[slot, 0:rows, :] = picked(lambda b: q_ref[pl.ds(b * rows, rows), :])
        stage[slot, rows : 2 * rows, :] = picked(lambda b: g_ref[pl.ds(b * rows, rows), :])
        stage[slot, 2 * rows : 2 * rows + 8, :] = picked(lambda b: meta[b])
        stage[slot, 2 * rows + 2 : 2 * rows + 3, :] = jnp.full(
            (1, heads * width), table_ref[slot, blocks]
        )

    pl.semaphore_wait(barrier, members + 2)
    remote(stage, x_arr, x_sems, 0, (partner, member)).start()
    for slot in range(1, members):
        remote(stage, m_arr, m_sems, slot, member_of(slot)).start()

    for h in range(heads):
        cols = pl.ds(h * width, width)
        kh, kl = split(k_ref[:, cols])
        kcat[h, :, 0:width] = kh
        kcat[h, :, width : 2 * width] = kl
        vh, vl = split(v_ref[:, cols])
        vcat[h, :, 0:width] = vh
        vcat[h, :, width : 2 * width] = vl
        th, tl = split(k_ref[:, cols].T)
        ktcat[h, 0:width, :] = th
        ktcat[h, width : 2 * width, :] = tl
    dk_ref[...] = jnp.zeros_like(dk_ref)
    dv_ref[...] = jnp.zeros_like(dv_ref)

    def attend(q, g, lse, delta, h):
        cols = pl.ds(h * width, width)
        qh, ql = split(q)
        gh, gl = split(g)
        kh, vh = kcat[h, :, 0:width], vcat[h, :, 0:width]
        scores = dot_t(kcat[h], jnp.concatenate([qh, qh], axis=1)) + dot_t(kh, ql)
        weights = jnp.exp(scores * scale - lse)
        prob_grads = dot_t(vcat[h], jnp.concatenate([gh, gh], axis=1)) + dot_t(vh, gl)
        score_grads = weights * (prob_grads - delta)
        ph, plow = split(weights)
        dv_ref[:, cols] += dot(jnp.concatenate([ph, plow], axis=1), jnp.concatenate([gh, gh], axis=0)) + dot(ph, gl)
        sh, sl = split(score_grads)
        dk_ref[:, cols] += dot(jnp.concatenate([sh, sl], axis=1), jnp.concatenate([qh, qh], axis=0)) + dot(sh, ql)
        kth, ktl = ktcat[h, 0:width, :], ktcat[h, width : 2 * width, :]
        dqt = dot(kth, sh) + dot(ktl, sh) + dot(kth, sl)
        return dqt.T * scale

    def own_block(b):
        here = pl.ds(pl.multiple_of(b * rows, rows), rows)
        for h in range(heads):
            cols = pl.ds(h * width, width)
            dq_ref[here, cols] = attend(
                q_ref[here, cols], g_ref[here, cols], meta[b, 0:1, cols], meta[b, 1:2, cols], h
            )

    def forward_member(slot):
        remote(stage, m_arr, m_sems, slot, member_of(slot)).wait_recv()
        remote(m_arr, x_arr, x_sems, slot, (partner, member)).start()

    def forward_far(slot):
        remote(stage, x_arr, x_sems, slot, (partner, member)).wait_recv()
        remote(x_arr, z_arr, z_sems, slot, (far_to, member)).start()

    own_block(0)
    for slot in range(1, members):
        forward_member(slot)
        if slot == 1:
            forward_far(0)
        if slot < blocks:
            own_block(slot)
    for b in range(max(members, 1), blocks):
        own_block(b)

    def local_of(slot):
        return stage if slot == 0 else m_arr

    flag_row = 2 * rows + 2

    def return_far(slot):
        remote(dq_slot, z_ret, zr_sems, slot, (far_from, member)).wait_recv()
        flag = local_of(slot)[slot, flag_row : flag_row + 1, :]
        x_out[slot] = jnp.where(flag == near_flag, dq_slot[slot], z_ret[slot])
        remote(x_out, x_ret, xr_sems, slot, (partner, member)).start()

    def return_near(slot):
        remote(x_out, x_ret, xr_sems, slot, (partner, member)).wait_recv()
        flag = local_of(slot)[slot, flag_row : flag_row + 1, :]
        total = jnp.where(flag == 0.0, dq_slot[slot], x_ret[slot])
        if slot == 0:
            m_ret[0] = total
        else:
            m_out[slot] = total
            remote(m_out, m_ret, mr_sems, slot, member_of(slot)).start()

    for slot in range(members):
        if slot + 1 < members:
            forward_far(slot + 1)
        remote(x_arr, z_arr, z_sems, slot, (far_to, member)).wait_recv()
        local = local_of(slot)
        flag = local[slot, flag_row : flag_row + 1, :]
        item[...] = jnp.where(
            flag == 0.0, local[slot], jnp.where(flag == near_flag, x_arr[slot], z_arr[slot])
        )
        for h in range(heads):
            cols = pl.ds(h * width, width)
            lse = jnp.where(flag[:, 0:width] == UNLISTED, 1e30, item[2 * rows : 2 * rows + 1, cols])
            dq_slot[slot, :, cols] = attend(
                item[0:rows, cols], item[rows : 2 * rows, cols], lse,
                item[2 * rows + 1 : 2 * rows + 2, cols], h,
            )
        remote(dq_slot, z_ret, zr_sems, slot, (far_from, member)).start()
        if slot >= 1:
            return_far(slot - 1)
        if slot >= 2:
            return_near(slot - 2)
    dk_ref[...] = dk_ref[...] * scale
    return_far(members - 1)
    for slot in range(max(members - 2, 0), members):
        return_near(slot)
    for slot in range(members):
        if slot >= 1:
            remote(m_out, m_ret, mr_sems, slot, member_of(slot)).wait_recv()
        for b in range(blocks):
            here = pl.ds(b * rows, rows)
            dq_ref[here, :] += m_ret[slot] * table_ref[slot, b]

    for slot in range(members):
        remote(local_of(slot), x_arr, x_sems, slot, (partner, member)).wait_send()
        remote(x_arr, z_arr, z_sems, slot, (far_to, member)).wait_send()
        remote(dq_slot, z_ret, zr_sems, slot, (far_from, member)).wait_send()
        remote(x_out, x_ret, xr_sems, slot, (partner, member)).wait_send()
        if slot >= 1:
            remote(stage, m_arr, m_sems, slot, member_of(slot)).wait_send()
            remote(m_out, m_ret, mr_sems, slot, member_of(slot)).wait_send()


def slot_table(block_lists, groups, members):
    blocks = block_lists.shape[0]
    group, member = lax.axis_index("group"), lax.axis_index("member")
    target = member ^ jnp.arange(members, dtype=jnp.int32)
    device = block_lists[:, blocks:] // blocks
    hit = (device % members)[None] == target[:, None, None]
    offset = (device // members - group + 1 + groups) % groups - 1
    flag = jnp.max(jnp.where(hit, offset[None], -groups), axis=(1, 2))
    flag = jnp.where(flag == -groups, UNLISTED, flag.astype(jnp.float32))
    return jnp.concatenate([jnp.any(hit, axis=2).astype(jnp.float32), flag[:, None]], axis=1)


def body(queries, keys, values, outputs, out_grads, log_sums, block_lists):
    tokens, width_all = queries.shape
    heads = log_sums.shape[1]
    blocks = block_lists.shape[0]
    rows, width = tokens // blocks, width_all // heads
    groups, members = lax.axis_size("group"), lax.axis_size("member")
    sizes = (groups, members, heads, width, blocks, rows)
    vmem = pl.BlockSpec(memory_space=pltpu.VMEM)
    packed = pltpu.VMEM((members, 2 * rows + 8, width_all), jnp.float32)
    terms = pltpu.VMEM((members, rows, width_all), jnp.float32)
    sems = pltpu.SemaphoreType.DMA((2, members))
    return pl.pallas_call(
        functools.partial(kernel, sizes),
        out_shape=[jax.ShapeDtypeStruct((tokens, width_all), jnp.float32)] * 3,
        in_specs=[pl.BlockSpec(memory_space=pltpu.SMEM)] + [vmem] * 6,
        out_specs=[vmem] * 3,
        scratch_shapes=[
            pltpu.VMEM((heads, tokens, 2 * width), jnp.bfloat16),
            pltpu.VMEM((heads, tokens, 2 * width), jnp.bfloat16),
            pltpu.VMEM((heads, 2 * width, tokens), jnp.bfloat16),
            pltpu.VMEM((blocks, 8, width_all), jnp.float32),
            packed, packed, packed, packed,
            pltpu.VMEM((2 * rows + 8, width_all), jnp.float32),
            terms, terms, terms, terms, terms, terms,
            sems, sems, sems, sems, sems, sems,
        ],
        compiler_params=pltpu.CompilerParams(
            collective_id=0, has_side_effects=True, vmem_limit_bytes=60 * 1024 * 1024
        ),
    )(slot_table(block_lists, groups, members), queries, keys, values, outputs, out_grads, log_sums)


def solution(mesh):
    spec = P(("group", "member"), None)
    return jax.shard_map(
        body, mesh=mesh, in_specs=(spec,) * 7, out_specs=(spec,) * 3, check_vma=False
    )
```

time: 169 us -> 71.5 us (0.42)
  Pallas kernels: 0 us -> 63.7 us
  starting transfers between devices: 54.6 us -> 0 us
  matrix products: 42.2 us -> 0 us
  local copies, waits for them, and re-layouts: 41.2 us -> 5.6 us
  waiting for transfers between devices: 26 us -> 0 us
    pallas_call x0 -> x1, Pallas kernels: none -> 63.7 us  [body(): pl.pallas_call(functools.partial(kernel, sizes), out_shape=[jax.ShapeDtyp...]
    dot_general x15 -> x0, matrix products: 42.2 us -> none  [the longest x2 8.2 us: one_step(): jnp.einsum('sqhd,khd->shqk', piece_grad, value_local, precision=exact_mode)]
    ppermute x12 -> x0, starting transfers between devices: 31.8 us -> none  [the longest x5 25 us: padded(): lax.ppermute(lax.slice_in_dim(block, 0, width, axis=dim), axis, backward)]
    ppermute x12 -> x0, waiting for transfers between devices: 25.5 us -> none  [the longest x5 11.5 us: padded(): lax.ppermute(lax.slice_in_dim(block, 0, width, axis=dim), axis, backward)]
    all_to_all x6 -> x0, starting transfers between devices: 22.8 us -> none  [the longest x1 4.42 us: body(): lax.all_to_all(query_slots, 'member', split_axis=1, concat_axis=1, tiled=...]
    concatenate x12 -> x0, local copies, waits for them, and re-layouts: 12.6 us -> none  [padded(): block = jnp.concatenate([low, block, high], axis=dim)]
    squeeze x7 -> x0, local copies, waits for them, and re-layouts: 7.55 us -> none  [the longest x6 6.28 us: body(): lax.map(one_item, (item_query, item_grad, item_lse, item_delta, item_flags))]
    reshape x5 -> x0, local copies, waits for them, and re-layouts: 4.96 us -> none  [the longest x2 2.31 us: body(): key_local = keys.reshape(row_count, head_count, head_dim)]
  transfers between devices with their start and end apart: 18 -> 0, of which waited for: 5 -> 0; matrix products, arithmetic and copies ran while one was open for 40% -> 0% of each run, Pallas kernels for 0% -> 0%
where the time goes in v1:
time: 71.5 us; the launch traced here: 71.2 us
  Pallas kernels  63.7 us (89%)
  local copies, waits for them, and re-layouts  5.6 us (8%)
  other arithmetic  1.22 us (2%)
    pallas_call x1, Pallas kernels, body(): pl.pallas_call(functools.partial(kernel, sizes), out_shape=[jax.ShapeDtyp...  63.7 us
    unnamed x12, local copies, waits for them, and re-layouts  5.5 us

profile of v1, /device:TPU:0, one launch (start us, length us, event | category | flops | bytes accessed | tf_op | source)
XLA Modules:
  0.0 71.2 jit_solution(2232018783627041535)
XLA Ops:
  0.6 0.0 copy-start.3
  0.7 0.7 copy-done.3
  1.3 0.1 add_select_fusion.2
  1.4 0.2 fusion
  1.6 0.2 compare_reduce_fusion
  1.9 0.1 copy.12
  2.0 0.0 copy-start.2
  2.0 0.7 pad_maximum_fusion.table_ref
  2.6 0.0 copy-done.2
  2.7 0.9 %copy.13.lse_ref = f32[512,2]{1,0:T(8,128)} copy(f32[512,2]{0,1:T(2,128)S(1)} %copy-done.2) | data formatting | bytes 8192 | tf_op args[5]
  3.5 63.7 %shard_map.94 = (f32[512,256]{1,0:T(8,128)}, f32[512,256]{1,0:T(8,128)}, f32[512,256]{1,0:T(8,128)}) custom-call(f32[4,5]{1,0:T(4,128)} %pad_maximum_fusion.table_ref, f32[512,256]{1,0:T(8,128)} %q_ref.1, f32[512,256]{1,0:T(8,128)} %k_ref.1, f32[512,256]{1,0:T(8,128)} %v_ref.1, f32[512,256]{1,0:T(8,128)} %o_ref.1, f32[512,256]{1,0:T(8,128)} %g_ref.1, ...), custom_call_target="tpu_custom_call" | custom-call | tf_op jit(solution)/shard_map/pallas_call | solution.py:242
  67.3 0.0 copy-start.1
  67.3 1.9 %copy.17 = f32[512,256]{1,0:T(8,128)} copy(f32[512,256]{1,0:T(8,128)} %get-tuple-element.8) | data formatting | bytes 1048576
  69.2 0.0 copy-done.1
  69.2 0.0 copy-start
  69.2 0.8 %copy.18 = f32[512,256]{1,0:T(8,128)} copy(f32[512,256]{1,0:T(8,128)S(1)} %copy-done.1) | data formatting | bytes 1048576
  70.0 0.4 copy-done
  70.4 0.8 %copy.19 = f32[512,256]{1,0:T(8,128)} copy(f32[512,256]{1,0:T(8,128)S(1)} %copy-done) | data formatting | bytes 1048576
  (3 shorter events, 0.0 us)
Async XLA Ops:
  0.6 0.7 copy-start.3
  2.0 0.7 copy-start.2
  67.3 1.9 %copy-start.1 = (f32[512,256]{1,0:T(8,128)S(1)}, f32[512,256]{1,0:T(8,128)}, u32[]{:S(2)}) copy-start(f32[512,256]{1,0:T(8,128)} %get-tuple-element.9) | copy-start | bytes 1572868
  69.2 1.2 %copy-start = (f32[512,256]{1,0:T(8,128)S(1)}, f32[512,256]{1,0:T(8,128)}, u32[]{:S(2)}) copy-start(f32[512,256]{1,0:T(8,128)} %get-tuple-element.10) | copy-start | bytes 1572868

commit v2 on v1

v2 whole, which is shorter than its diff:
```python
import functools

import jax
import jax.numpy as jnp
from jax import lax
from jax.experimental import pallas as pl
from jax.experimental.pallas import tpu as pltpu
from jax.sharding import PartitionSpec as P

MESH = pl.DeviceIdType.MESH
UNLISTED = 2.0


def split(x):
    high = x.astype(jnp.bfloat16)
    return high, (x - high.astype(jnp.float32)).astype(jnp.bfloat16)


def dot(a, b):
    return lax.dot_general(a, b, (((1,), (0,)), ((), ())), preferred_element_type=jnp.float32)


def dot_t(a, b):
    return lax.dot_general(a, b, (((1,), (1,)), ((), ())), preferred_element_type=jnp.float32)


def xor_index(a, b, count):
    total, bit = 0, 1
    while bit < count:
        total = total + ((a // bit + b // bit) % 2) * bit
        bit *= 2
    return total


def kernel(
    sizes, table_ref, q_ref, k_hbm, v_hbm, o_ref, g_ref, lse_ref, dq_ref, dk_ref, dv_ref,
    k_ref, v_ref, kcat, vcat, ktcat, meta, stage, m_arr, x_arr, z_arr, item,
    dq_item, z_ret, x_out, x_ret, m_out, m_ret,
    kv_sems, m_sems, x_sems, z_sems, zr_sems, xr_sems, mr_sems,
):
    groups, members, heads, width, blocks, rows = sizes
    scale = width ** -0.5
    group, member = lax.axis_index("group"), lax.axis_index("member")
    parity = group % 2
    partner = group + 1 - 2 * parity
    far_to = (group + 2 - 4 * parity + groups) % groups
    far_from = (group - 2 + 4 * parity + groups) % groups
    near_flag = (2 * parity - 1).astype(jnp.float32)

    barrier = pltpu.get_barrier_semaphore()
    for other in (partner, far_to, far_from):
        pl.semaphore_signal(barrier, inc=1, device_id=(other, member), device_id_type=MESH)
    for step in range(1, members):
        pl.semaphore_signal(
            barrier, inc=1, device_id=(group, xor_index(member, step, members)), device_id_type=MESH
        )
    kv_copies = [
        pltpu.make_async_copy(k_hbm, k_ref, kv_sems.at[0]),
        pltpu.make_async_copy(v_hbm, v_ref, kv_sems.at[1]),
    ]
    for copy in kv_copies:
        copy.start()

    slots = [0] + list(range(2, members)) + list(range(1, min(members, 2)))
    items = [(slot, h) for slot in slots for h in range(heads)]
    count = len(items)

    def remote(source, target, sems, n, device):
        return pltpu.make_async_remote_copy(
            src_ref=source.at[n], dst_ref=target.at[n],
            send_sem=sems.at[0, n], recv_sem=sems.at[1, n],
            device_id=device, device_id_type=MESH,
        )

    def to_member(source, target, sems, n):
        return remote(source, target, sems, n, (group, xor_index(member, items[n][0], members)))

    def to_partner(source, target, sems, n):
        return remote(source, target, sems, n, (partner, member))

    eye = lax.broadcasted_iota(jnp.int32, (rows, rows), 0) == lax.broadcasted_iota(
        jnp.int32, (rows, rows), 1
    )
    for b in range(blocks):
        here = pl.ds(b * rows, rows)
        for h in range(heads):
            cols = pl.ds(h * width, width)
            delta = jnp.sum(g_ref[here, cols] * o_ref[here, cols], axis=1, keepdims=True)
            meta[b, h, 0:1, :] = lse_ref[h : h + 1, here]
            meta[b, h, 1:2, :] = jnp.sum(jnp.where(eye, delta, 0.0), axis=0, keepdims=True)

    def fill(n):
        slot, h = items[n]
        cols = pl.ds(h * width, width)

        def picked(read):
            return sum(read(b) * table_ref[slot, b] for b in range(blocks))

        stage[n, 0:rows, :] = picked(lambda b: q_ref[pl.ds(b * rows, rows), cols])
        stage[n, rows : 2 * rows, :] = picked(lambda b: g_ref[pl.ds(b * rows, rows), cols])
        stage[n, 2 * rows : 2 * rows + 2, :] = picked(lambda b: meta[b, h, 0:2, :])
        stage[n, 2 * rows + 2 : 2 * rows + 8, :] = jnp.full((6, width), table_ref[slot, blocks])

    for n in range(count):
        if n <= heads:
            fill(n)
    pl.semaphore_wait(barrier, members + 2)
    for n in range(count):
        if n > heads:
            fill(n)
        if items[n][0] == 0:
            to_partner(stage, x_arr, x_sems, n).start()
        else:
            to_member(stage, m_arr, m_sems, n).start()

    for copy in kv_copies:
        copy.wait()
    for h in range(heads):
        cols = pl.ds(h * width, width)
        kh, kl = split(k_ref[:, cols])
        kcat[h, :, 0:width] = kh
        kcat[h, :, width : 2 * width] = kl
        vh, vl = split(v_ref[:, cols])
        vcat[h, :, 0:width] = vh
        vcat[h, :, width : 2 * width] = vl
        th, tl = split(k_ref[:, cols].T)
        ktcat[h, 0:width, :] = th
        ktcat[h, width : 2 * width, :] = tl
    dk_ref[...] = jnp.zeros_like(dk_ref)
    dv_ref[...] = jnp.zeros_like(dv_ref)

    def attend(q, g, lse, delta, h):
        cols = pl.ds(h * width, width)
        qh, ql = split(q)
        gh, gl = split(g)
        kh, vh = kcat[h, :, 0:width], vcat[h, :, 0:width]
        scores = dot_t(kcat[h], jnp.concatenate([qh, qh], axis=1)) + dot_t(kh, ql)
        weights = jnp.exp(scores * scale - lse)
        prob_grads = dot_t(vcat[h], jnp.concatenate([gh, gh], axis=1)) + dot_t(vh, gl)
        score_grads = weights * (prob_grads - delta)
        ph, plow = split(weights)
        dv_ref[:, cols] += dot(
            jnp.concatenate([ph, plow], axis=1), jnp.concatenate([gh, gh], axis=0)
        ) + dot(ph, gl)
        sh, sl = split(score_grads)
        dk_ref[:, cols] += dot(
            jnp.concatenate([sh, sl], axis=1), jnp.concatenate([qh, qh], axis=0)
        ) + dot(sh, ql)
        kth, ktl = ktcat[h, 0:width, :], ktcat[h, width : 2 * width, :]
        return (dot(kth, sh) + dot(ktl, sh) + dot(kth, sl)).T * scale

    def own_unit(unit):
        b, h = unit // heads, unit % heads
        here, cols = pl.ds(b * rows, rows), pl.ds(h * width, width)
        dq_ref[here, cols] = attend(
            q_ref[here, cols], g_ref[here, cols], meta[b, h, 0:1, :], meta[b, h, 1:2, :], h
        )

    def local_of(n):
        return stage if items[n][0] == 0 else m_arr

    def flag_of(n):
        return local_of(n)[n, 2 * rows + 2 : 2 * rows + 3, :]

    def forward_member(n):
        if items[n][0] != 0:
            to_member(stage, m_arr, m_sems, n).wait_recv()
            to_partner(m_arr, x_arr, x_sems, n).start()

    def forward_far(n):
        to_partner(stage, x_arr, x_sems, n).wait_recv()
        remote(x_arr, z_arr, z_sems, n, (far_to, member)).start()

    def compute(n):
        remote(x_arr, z_arr, z_sems, n, (far_to, member)).wait_recv()
        flag = flag_of(n)
        item[...] = jnp.where(
            flag == 0.0, local_of(n)[n], jnp.where(flag == near_flag, x_arr[n], z_arr[n])
        )
        lse = jnp.where(flag == UNLISTED, 1e30, item[2 * rows : 2 * rows + 1, :])
        dq_item[n] = attend(
            item[0:rows, :], item[rows : 2 * rows, :], lse,
            item[2 * rows + 1 : 2 * rows + 2, :], items[n][1],
        )
        remote(dq_item, z_ret, zr_sems, n, (far_from, member)).start()

    def return_far(n):
        remote(dq_item, z_ret, zr_sems, n, (far_from, member)).wait_recv()
        x_out[n] = jnp.where(flag_of(n) == near_flag, dq_item[n], z_ret[n])
        to_partner(x_out, x_ret, xr_sems, n).start()

    def return_near(n):
        to_partner(x_out, x_ret, xr_sems, n).wait_recv()
        total = jnp.where(flag_of(n) == 0.0, dq_item[n], x_ret[n])
        if items[n][0] == 0:
            m_ret[n] = total
        else:
            m_out[n] = total
            to_member(m_out, m_ret, mr_sems, n).start()

    def finish(n):
        slot, h = items[n]
        if slot != 0:
            to_member(m_out, m_ret, mr_sems, n).wait_recv()
        for b in range(blocks):
            here, cols = pl.ds(b * rows, rows), pl.ds(h * width, width)
            dq_ref[here, cols] += m_ret[n] * table_ref[slot, b]

    units = blocks * heads
    stages = ((forward_member, -1), (forward_far, 1), (compute, 2), (return_far, 4), (return_near, 6), (finish, 8))
    for step in range(-1, max(count + 9, units)):
        if 0 <= step < units:
            own_unit(step)
        for stage_of, lag in stages:
            if 0 <= step - lag < count:
                stage_of(step - lag)
        if step == count + 1:
            dk_ref[...] = dk_ref[...] * scale

    for n in range(count):
        to_partner(local_of(n), x_arr, x_sems, n).wait_send()
        remote(x_arr, z_arr, z_sems, n, (far_to, member)).wait_send()
        remote(dq_item, z_ret, zr_sems, n, (far_from, member)).wait_send()
        to_partner(x_out, x_ret, xr_sems, n).wait_send()
        if items[n][0] != 0:
            to_member(stage, m_arr, m_sems, n).wait_send()
            to_member(m_out, m_ret, mr_sems, n).wait_send()


def slot_table(block_lists, groups, members):
    blocks = block_lists.shape[0]
    group, member = lax.axis_index("group"), lax.axis_index("member")
    target = member ^ jnp.arange(members, dtype=jnp.int32)
    device = block_lists[:, blocks:] // blocks
    hit = (device % members)[None] == target[:, None, None]
    offset = (device // members - group + 1 + groups) % groups - 1
    flag = jnp.max(jnp.where(hit, offset[None], -groups), axis=(1, 2))
    flag = jnp.where(flag == -groups, UNLISTED, flag.astype(jnp.float32))
    return jnp.concatenate([jnp.any(hit, axis=2).astype(jnp.float32), flag[:, None]], axis=1)


def body(queries, keys, values, outputs, out_grads, log_sums, block_lists):
    tokens, width_all = queries.shape
    heads = log_sums.shape[1]
    blocks = block_lists.shape[0]
    rows, width = tokens // blocks, width_all // heads
    groups, members = lax.axis_size("group"), lax.axis_size("member")
    sizes = (groups, members, heads, width, blocks, rows)
    vmem = pl.BlockSpec(memory_space=pltpu.VMEM)
    anywhere = pl.BlockSpec(memory_space=pl.ANY)
    count = members * heads
    packed = pltpu.VMEM((count, 2 * rows + 8, width), jnp.float32)
    terms = pltpu.VMEM((count, rows, width), jnp.float32)
    sems = pltpu.SemaphoreType.DMA((2, count))
    return pl.pallas_call(
        functools.partial(kernel, sizes),
        out_shape=[jax.ShapeDtypeStruct((tokens, width_all), jnp.float32)] * 3,
        in_specs=[pl.BlockSpec(memory_space=pltpu.SMEM), vmem, anywhere, anywhere, vmem, vmem, vmem],
        out_specs=[vmem] * 3,
        scratch_shapes=[
            pltpu.VMEM((tokens, width_all), jnp.float32),
            pltpu.VMEM((tokens, width_all), jnp.float32),
            pltpu.VMEM((heads, tokens, 2 * width), jnp.bfloat16),
            pltpu.VMEM((heads, tokens, 2 * width), jnp.bfloat16),
            pltpu.VMEM((heads, 2 * width, tokens), jnp.bfloat16),
            pltpu.VMEM((blocks, heads, 8, width), jnp.float32),
            packed, packed, packed, packed,
            pltpu.VMEM((2 * rows + 8, width), jnp.float32),
            terms, terms, terms, terms, terms, terms,
            pltpu.SemaphoreType.DMA((2,)),
            sems, sems, sems, sems, sems, sems,
        ],
        compiler_params=pltpu.CompilerParams(
            collective_id=0, has_side_effects=True, vmem_limit_bytes=60 * 1024 * 1024
        ),
    )(slot_table(block_lists, groups, members), queries, keys, values, outputs, out_grads, log_sums.T)


def solution(mesh):
    spec = P(("group", "member"), None)
    return jax.shard_map(
        body, mesh=mesh, in_specs=(spec,) * 7, out_specs=(spec,) * 3, check_vma=False
    )
```

time: 71.5 us -> 65.1 us (0.910)
  Pallas kernels: 63.7 us -> 58.3 us
  local copies, waits for them, and re-layouts: 5.6 us -> 4.71 us
    pallas_call x1, Pallas kernels: 63.7 us -> 58.3 us  [body(): pl.pallas_call(functools.partial(kernel, sizes), out_shape=[jax.ShapeDtyp...]
    unnamed x12 -> x9, local copies, waits for them, and re-layouts: 5.5 us -> 4.62 us
where the time goes in v2:
time: 65.1 us; the launch traced here: 64.9 us
  Pallas kernels  58.3 us (90%)
  local copies, waits for them, and re-layouts  4.71 us (7%)
  other arithmetic  1.22 us (2%)
  between operations  0.68 us (1%)
    pallas_call x1, Pallas kernels, body(): pl.pallas_call(functools.partial(kernel, sizes), out_shape=[jax.ShapeDtyp...  58.3 us
    unnamed x9, local copies, waits for them, and re-layouts  4.62 us

profile of v2, /device:TPU:0, one launch (start us, length us, event | category | flops | bytes accessed | tf_op | source)
XLA Modules:
  0.0 64.9 jit_solution(3958818794254476001)
XLA Ops:
  0.6 0.0 copy-start.2
  0.7 0.7 %copy-done.2 = s32[4,8]{1,0:T(4,128)S(1)} copy-done((s32[4,8]{1,0:T(4,128)S(1)}, s32[4,8]{1,0:T(4,128)}, u32[]{:S(2)}) %copy-start.2) | copy-done | bytes 152
  1.3 0.1 add_select_fusion.2
  1.4 0.2 fusion
  1.6 0.2 compare_reduce_fusion
  1.9 0.1 copy.11
  2.0 0.7 %pad_maximum_fusion.table_ref = f32[4,5]{1,0:T(4,128)} fusion(f32[4,1]{1,0:T(4,128)S(1)} %copy.11, f32[4,4]{1,0:T(4,128)S(1)} %convert_element_type.14), kind=kLoop, calls=%fused_computation.20 | loop fusion | flops 20 | bytes 160 | tf_op jit(solution)/shard_map/concatenate | solution.py:239
  2.6 58.3 %shard_map.94 = (f32[512,256]{1,0:T(8,128)}, f32[512,256]{1,0:T(8,128)}, f32[512,256]{1,0:T(8,128)}) custom-call(f32[4,5]{1,0:T(4,128)} %pad_maximum_fusion.table_ref, f32[512,256]{1,0:T(8,128)} %q_ref.1, f32[512,256]{1,0:T(8,128)} %k_hbm.1, f32[512,256]{1,0:T(8,128)} %v_hbm.1, f32[512,256]{1,0:T(8,128)} %o_ref.1, f32[512,256]{1,0:T(8,128)} %g_ref.1, ...), custom_call_target="tpu_custom_call" | custom-call | tf_op jit(solution)/shard_map/pallas_call | solution.py:255
  60.9 0.0 copy-start.1
  60.9 1.9 %copy.15 = f32[512,256]{1,0:T(8,128)} copy(f32[512,256]{1,0:T(8,128)} %get-tuple-element.8) | data formatting | bytes 1048576
  62.9 0.0 copy-done.1
  62.9 0.0 copy-start
  62.9 0.8 %copy.16 = f32[512,256]{1,0:T(8,128)} copy(f32[512,256]{1,0:T(8,128)S(1)} %copy-done.1) | data formatting | bytes 1048576
  63.7 0.4 copy-done
  64.1 0.8 %copy.17 = f32[512,256]{1,0:T(8,128)} copy(f32[512,256]{1,0:T(8,128)S(1)} %copy-done) | data formatting | bytes 1048576
  (3 shorter events, 0.0 us)
Async XLA Ops:
  0.6 0.7 %copy-start.2 = (s32[4,8]{1,0:T(4,128)S(1)}, s32[4,8]{1,0:T(4,128)}, u32[]{:S(2)}) copy-start(s32[4,8]{1,0:T(4,128)} %param.13) | copy-start | bytes 388
  60.9 1.9 %copy-start.1 = (f32[512,256]{1,0:T(8,128)S(1)}, f32[512,256]{1,0:T(8,128)}, u32[]{:S(2)}) copy-start(f32[512,256]{1,0:T(8,128)} %get-tuple-element.9) | copy-start | bytes 1572868
  62.9 1.2 %copy-start = (f32[512,256]{1,0:T(8,128)S(1)}, f32[512,256]{1,0:T(8,128)}, u32[]{:S(2)}) copy-start(f32[512,256]{1,0:T(8,128)} %get-tuple-element.10) | copy-start | bytes 1572868

commit v3 on v2

--- a/solution.py
+++ b/solution.py
@@ -33,12 +33,13 @@
 
 
 def kernel(
-    sizes, table_ref, q_ref, k_hbm, v_hbm, o_ref, g_ref, lse_ref, dq_ref, dk_ref, dv_ref,
-    k_ref, v_ref, kcat, vcat, ktcat, meta, stage, m_arr, x_arr, z_arr, item,
+    sizes, lists_ref, q_hbm, k_hbm, v_hbm, o_hbm, g_hbm, lse_ref, dq_ref, dk_ref, dv_ref,
+    q_ref, o_ref, g_ref, k_ref, v_ref, kcat, vcat, ktcat, meta, stage, m_arr, x_arr, z_arr, item,
     dq_item, z_ret, x_out, x_ret, m_out, m_ret,
     kv_sems, m_sems, x_sems, z_sems, zr_sems, xr_sems, mr_sems,
 ):
     groups, members, heads, width, blocks, rows = sizes
+    factors, flags = {}, {}
     scale = width ** -0.5
     group, member = lax.axis_index("group"), lax.axis_index("member")
     parity = group % 2
@@ -54,6 +55,13 @@
         pl.semaphore_signal(
             barrier, inc=1, device_id=(group, xor_index(member, step, members)), device_id_type=MESH
         )
+    early_copies = [
+        pltpu.make_async_copy(g_hbm, g_ref, kv_sems.at[2]),
+        pltpu.make_async_copy(o_hbm, o_ref, kv_sems.at[3]),
+        pltpu.make_async_copy(q_hbm, q_ref, kv_sems.at[4]),
+    ]
+    for copy in early_copies:
+        copy.start()
     kv_copies = [
         pltpu.make_async_copy(k_hbm, k_ref, kv_sems.at[0]),
         pltpu.make_async_copy(v_hbm, v_ref, kv_sems.at[1]),
@@ -77,6 +85,26 @@
 
     def to_partner(source, target, sems, n):
         return remote(source, target, sems, n, (partner, member))
+
+    listed = lists_ref.shape[1]
+    for slot in range(members):
+        target = xor_index(member, slot, members)
+        flag = jnp.int32(-groups)
+        for b in range(blocks):
+            hits = jnp.int32(0)
+            for entry in range(blocks, listed):
+                device = lax.div(lists_ref[b, entry], jnp.int32(blocks))
+                hit = lax.rem(device, jnp.int32(members)) == target
+                offset = lax.rem(
+                    lax.div(device, jnp.int32(members)) - group + 1 + groups, jnp.int32(groups)
+                ) - 1
+                hits = jnp.maximum(hits, hit.astype(jnp.int32))
+                flag = jnp.maximum(flag, jnp.where(hit, offset, -groups))
+            factors[slot, b] = hits.astype(jnp.float32)
+        flags[slot] = jnp.where(flag == -groups, UNLISTED, flag.astype(jnp.float32))
+
+    for copy in early_copies:
+        copy.wait()
 
     eye = lax.broadcasted_iota(jnp.int32, (rows, rows), 0) == lax.broadcasted_iota(
         jnp.int32, (rows, rows), 1
@@ -94,12 +122,12 @@
         cols = pl.ds(h * width, width)
 
         def picked(read):
-            return sum(read(b) * table_ref[slot, b] for b in range(blocks))
+            return sum(read(b) * factors[slot, b] for b in range(blocks))
 
         stage[n, 0:rows, :] = picked(lambda b: q_ref[pl.ds(b * rows, rows), cols])
         stage[n, rows : 2 * rows, :] = picked(lambda b: g_ref[pl.ds(b * rows, rows), cols])
         stage[n, 2 * rows : 2 * rows + 2, :] = picked(lambda b: meta[b, h, 0:2, :])
-        stage[n, 2 * rows + 2 : 2 * rows + 8, :] = jnp.full((6, width), table_ref[slot, blocks])
+        stage[n, 2 * rows + 2 : 2 * rows + 8, :] = jnp.full((6, width), flags[slot])
 
     for n in range(count):
         if n <= heads:
@@ -204,7 +232,7 @@
             to_member(m_out, m_ret, mr_sems, n).wait_recv()
         for b in range(blocks):
             here, cols = pl.ds(b * rows, rows), pl.ds(h * width, width)
-            dq_ref[here, cols] += m_ret[n] * table_ref[slot, b]
+            dq_ref[here, cols] += m_ret[n] * factors[slot, b]
 
     units = blocks * heads
     stages = ((forward_member, -1), (forward_far, 1), (compute, 2), (return_far, 4), (return_near, 6), (finish, 8))
@@ -227,16 +255,13 @@
             to_member(m_out, m_ret, mr_sems, n).wait_send()
 
 
-def slot_table(block_lists, groups, members):
-    blocks = block_lists.shape[0]
-    group, member = lax.axis_index("group"), lax.axis_index("member")
-    target = member ^ jnp.arange(members, dtype=jnp.int32)
-    device = block_lists[:, blocks:] // blocks
-    hit = (device % members)[None] == target[:, None, None]
-    offset = (device // members - group + 1 + groups) % groups - 1
-    flag = jnp.max(jnp.where(hit, offset[None], -groups), axis=(1, 2))
-    flag = jnp.where(flag == -groups, UNLISTED, flag.astype(jnp.float32))
-    return jnp.concatenate([jnp.any(hit, axis=2).astype(jnp.float32), flag[:, None]], axis=1)
+def settle(a_in, b_in, c_in, a_out, b_out, c_out, sems):
+    pairs = ((a_in, a_out), (b_in, b_out), (c_in, c_out))
+    copies = [pltpu.make_async_copy(x, y, sems.at[n]) for n, (x, y) in enumerate(pairs)]
+    for copy in copies:
+        copy.start()
+    for copy in copies:
+        copy.wait()
 
 
 def body(queries, keys, values, outputs, out_grads, log_sums, block_lists):
@@ -252,12 +277,15 @@
     packed = pltpu.VMEM((count, 2 * rows + 8, width), jnp.float32)
     terms = pltpu.VMEM((count, rows, width), jnp.float32)
     sems = pltpu.SemaphoreType.DMA((2, count))
-    return pl.pallas_call(
+    results = pl.pallas_call(
         functools.partial(kernel, sizes),
         out_shape=[jax.ShapeDtypeStruct((tokens, width_all), jnp.float32)] * 3,
-        in_specs=[pl.BlockSpec(memory_space=pltpu.SMEM), vmem, anywhere, anywhere, vmem, vmem, vmem],
+        in_specs=[pl.BlockSpec(memory_space=pltpu.SMEM), anywhere, anywhere, anywhere, anywhere, anywhere, vmem],
         out_specs=[vmem] * 3,
         scratch_shapes=[
+            pltpu.VMEM((tokens, width_all), jnp.float32),
+            pltpu.VMEM((tokens, width_all), jnp.float32),
+            pltpu.VMEM((tokens, width_all), jnp.float32),
             pltpu.VMEM((tokens, width_all), jnp.float32),
             pltpu.VMEM((tokens, width_all), jnp.float32),
             pltpu.VMEM((heads, tokens, 2 * width), jnp.bfloat16),
@@ -267,13 +295,21 @@
             packed, packed, packed, packed,
             pltpu.VMEM((2 * rows + 8, width), jnp.float32),
             terms, terms, terms, terms, terms, terms,
-            pltpu.SemaphoreType.DMA((2,)),
+            pltpu.SemaphoreType.DMA((5,)),
             sems, sems, sems, sems, sems, sems,
         ],
         compiler_params=pltpu.CompilerParams(
             collective_id=0, has_side_effects=True, vmem_limit_bytes=60 * 1024 * 1024
         ),
-    )(slot_table(block_lists, groups, members), queries, keys, values, outputs, out_grads, log_sums.T)
+    )(block_lists, queries, keys, values, outputs, out_grads, log_sums.T)
+    return pl.pallas_call(
+        settle,
+        out_shape=[jax.ShapeDtypeStruct((tokens, width_all), jnp.float32)] * 3,
+        in_specs=[vmem] * 3,
+        out_specs=[anywhere] * 3,
+        scratch_shapes=[pltpu.SemaphoreType.DMA((3,))],
+        compiler_params=pltpu.CompilerParams(vmem_limit_bytes=8 * 1024 * 1024),
+    )(*results)
 
 
 def solution(mesh):

time: 65.1 us -> 63 us (0.968)
  local copies, waits for them, and re-layouts: 4.71 us -> 3.12 us
  other arithmetic: 1.22 us -> 0 us
  Pallas kernels: 58.3 us -> 59 us
    unnamed x9 -> x6, local copies, waits for them, and re-layouts: 4.62 us -> 3.12 us
    pallas_call x0 -> x1, Pallas kernels: none -> 1.16 us  [body(): pl.pallas_call(settle, out_shape=[jax.ShapeDtypeStruct((tokens, width_all...]
    concatenate x1 -> x0, other arithmetic: 0.66 us -> none  [slot_table(): jnp.concatenate([jnp.any(hit, axis=2).astype(jnp.float32), flag[:, None]]...]
where the time goes in v3:
time: 63 us; the launch traced here: 62.7 us
  Pallas kernels  59 us (94%)
  local copies, waits for them, and re-layouts  3.12 us (5%)
  between operations  0.65 us (1%)
    pallas_call x1, Pallas kernels, body(): pl.pallas_call(functools.partial(kernel, sizes), out_shape=[jax.ShapeDtyp...  57.8 us
    unnamed x6, local copies, waits for them, and re-layouts  3.12 us

profile of v3, /device:TPU:0, one launch (start us, length us, event | category | flops | bytes accessed | tf_op | source)
XLA Modules:
  0.0 62.7 jit_solution(5317279622248377352)
XLA Ops:
  0.6 57.8 %shard_map.94 = (f32[512,256]{1,0:T(8,128)}, f32[512,256]{1,0:T(8,128)}, f32[512,256]{1,0:T(8,128)}) custom-call(s32[4,8]{1,0:T(4,128)} %lists_ref.1, f32[512,256]{1,0:T(8,128)} %q_hbm.1, f32[512,256]{1,0:T(8,128)} %k_hbm.1, f32[512,256]{1,0:T(8,128)} %v_hbm.1, f32[512,256]{1,0:T(8,128)} %o_hbm.1, f32[512,256]{1,0:T(8,128)} %g_hbm.1, f32[2,512]{1,0:T(2,128)} %bitcast.1), custom_call_target="tpu_custom_call" | custom-call | tf_op jit(solution)/shard_map/pallas_call | solution.py:280
  58.4 0.0 copy-start
  58.4 1.0 %copy-done = f32[512,256]{1,0:T(8,128)S(1)} copy-done((f32[512,256]{1,0:T(8,128)S(1)}, f32[512,256]{1,0:T(8,128)}, u32[]{:S(2)}) %copy-start) | copy-done | bytes 524312
  59.5 0.0 copy-start.1
  59.5 1.0 %copy-done.1 = f32[512,256]{1,0:T(8,128)S(1)} copy-done((f32[512,256]{1,0:T(8,128)S(1)}, f32[512,256]{1,0:T(8,128)}, u32[]{:S(2)}) %copy-start.1) | copy-done | bytes 524312
  60.5 0.0 copy-start.2
  60.5 1.0 %copy-done.2 = f32[512,256]{1,0:T(8,128)S(1)} copy-done((f32[512,256]{1,0:T(8,128)S(1)}, f32[512,256]{1,0:T(8,128)}, u32[]{:S(2)}) %copy-start.2) | copy-done | bytes 524312
  61.6 1.2 %shard_map.95 = (f32[512,256]{1,0:T(8,128)}, f32[512,256]{1,0:T(8,128)}, f32[512,256]{1,0:T(8,128)}) custom-call(f32[512,256]{1,0:T(8,128)S(1)} %copy-done, f32[512,256]{1,0:T(8,128)S(1)} %copy-done.1, f32[512,256]{1,0:T(8,128)S(1)} %copy-done.2), custom_call_target="tpu_custom_call" | custom-call | tf_op jit(solution)/shard_map/pallas_call | solution.py:305
Async XLA Ops:
  58.4 1.0 %copy-start = (f32[512,256]{1,0:T(8,128)S(1)}, f32[512,256]{1,0:T(8,128)}, u32[]{:S(2)}) copy-start(f32[512,256]{1,0:T(8,128)} %get-tuple-element.6.a_in) | copy-start | bytes 1572868
  59.5 1.0 %copy-start.1 = (f32[512,256]{1,0:T(8,128)S(1)}, f32[512,256]{1,0:T(8,128)}, u32[]{:S(2)}) copy-start(f32[512,256]{1,0:T(8,128)} %get-tuple-element.7.b_in) | copy-start | bytes 1572868
  60.5 1.0 %copy-start.2 = (f32[512,256]{1,0:T(8,128)S(1)}, f32[512,256]{1,0:T(8,128)}, u32[]{:S(2)}) copy-start(f32[512,256]{1,0:T(8,128)} %get-tuple-element.8.c_in) | copy-start | bytes 1572868
